TPU v7x, 256 devices: a whole 4x4x8 slice. The times are simulated.
256 devices in a mesh: dp: 16 (over y_hi, z), fsdp: 16 (over y_lo, x, core).
Axes of the slice: x: 4, y: 4 (y_hi: 2, y_lo: 2; y = y_hi * 2 + y_lo), z: 8, core: 2. Of those that a mesh axis runs over, the one named last changes fastest.
Arguments:
- item_tokens: bfloat16 [131072, 4096], P(('dp', 'fsdp')), may hold values from -6 to 6
- item_lengths: int32 [1024], P(('dp', 'fsdp')), may hold values from 1 to 128
- item_gain: float32 [4096], replicated, may hold values from 0.1 to 1.9
- user_source: int32 [65536, 1], P(('dp', 'fsdp')), may hold values from 0 to 15; in each aligned block of 256 rows (0 to 255, 256 to 511, ...) at most 24 rows name the same one
- user_slot: int32 [65536], P(('dp', 'fsdp')), may hold values from 0 to 3
- user_lengths: int32 [256], P(('dp', 'fsdp')), may hold values from 1 to 256
- user_gain: float32 [4096], replicated, may hold values from 0.1 to 1.9
- key_weight: bfloat16 [4096, 1024], P('fsdp'), may hold values from -0.09375 to 0.09375
- key_grad: bfloat16 [65536, 1024], P(('dp', 'fsdp')), may hold values from -6 to 6
Outputs:
- keys: bfloat16 [65536, 1024], P(('dp', 'fsdp'))
- weight_grad: float32 [4096, 1024], P('fsdp')
- token_grads: bfloat16 [131072, 4096], P(('dp', 'fsdp'))
Inputs may be any that keep to these rules, and one draw needn't show every extreme that they name: `user_source`: among the 256 positions of one device, no source index appears more than 24 times, and in every draw some device reaches 24 for some source.
All inputs are finite; a program needn't handle non-finite values.
Results may differ from a plain program's by a relative error of at most 0.0057.
Values may be sent and summed in bfloat16 or wider, within the bound.
A program may use at most 128 MiB of HBM per device.

v0:
```python
import jax
import jax.numpy as jnp
from jax import lax
from jax.sharding import PartitionSpec as P

EPS = 1e-05


def rms_scale(vector, gain_row):
    return vector * lax.rsqrt(jnp.mean(vector * vector, axis=-1, keepdims=True) + EPS) * gain_row


def pool_items(token_block, valid_mask, item_sizes, gain_row):
    normed = rms_scale(token_block, gain_row)
    return jnp.sum(normed * valid_mask[:, :, None], axis=1) / item_sizes[:, None]


def local(
    item_tokens,
    item_lengths,
    item_gain,
    user_source,
    user_slot,
    user_lengths,
    user_gain,
    key_weight,
    key_grad,
):
    item_count = item_lengths.shape[0]
    block_rows = item_tokens.shape[0] // item_count
    model_width = item_tokens.shape[1]
    group_count = lax.axis_size("dp")
    stacked_tokens = item_tokens.reshape(item_count, block_rows, model_width)
    valid_mask = (
        lax.broadcasted_iota(jnp.int32, (item_count, block_rows), 1) < item_lengths[:, None]
    ).astype(jnp.float32)
    item_sizes = item_lengths.astype(jnp.float32)

    def pooling(tokens_float):
        return pool_items(tokens_float, valid_mask, item_sizes, item_gain)

    pooled, pool_back = jax.vjp(pooling, stacked_tokens.astype(jnp.float32))
    item_emb = pooled.astype(jnp.bfloat16)
    weights = lax.all_gather(key_weight, "fsdp", axis=0, tiled=True)
    row_count = user_slot.shape[0]
    source = user_source[:, 0]
    seq_count = user_lengths.shape[0]
    seq_rows = row_count // seq_count
    alive_mask = (
        lax.broadcasted_iota(jnp.int32, (seq_count, seq_rows), 1) < user_lengths[:, None]
    ).reshape(row_count, 1)
    capacity = 3 * row_count // (2 * group_count)
    source_hot = (
        source[:, None] == lax.broadcasted_iota(jnp.int32, (row_count, group_count), 1)
    ).astype(jnp.int32)
    before = jnp.cumsum(source_hot, axis=0) - source_hot
    slot_rank = jnp.sum(before * source_hot, axis=1)
    bucket = source * capacity + slot_rank
    request = (
        jnp.zeros((group_count * capacity,), jnp.int32)
        .at[bucket]
        .set(user_slot)
        .reshape(group_count, capacity)
    )
    requested = lax.all_to_all(request, "dp", split_axis=0, concat_axis=0, tiled=True)
    outgoing = jnp.take(item_emb, requested.reshape(-1), axis=0).reshape(
        group_count, capacity, model_width
    )
    arrived = lax.all_to_all(outgoing, "dp", split_axis=0, concat_axis=0, tiled=True)
    fetched = jnp.take(arrived.reshape(group_count * capacity, model_width), bucket, axis=0)
    embedded = jnp.where(alive_mask, fetched, jnp.zeros_like(fetched))

    def normalize(vector):
        return rms_scale(vector, user_gain)

    scaled, norm_back = jax.vjp(normalize, embedded.astype(jnp.float32))
    hidden = scaled.astype(jnp.bfloat16)
    key_rows = jnp.dot(hidden, weights, preferred_element_type=jnp.float32).astype(jnp.bfloat16)
    hidden_grad = lax.dot_general(
        key_grad, weights, (((1,), (1,)), ((), ())), preferred_element_type=jnp.float32
    )
    (embed_grad,) = norm_back(hidden_grad)
    pos_grad = jnp.where(alive_mask, embed_grad, jnp.zeros_like(embed_grad)).astype(jnp.bfloat16)
    weight_shard = lax.psum_scatter(
        lax.dot_general(
            hidden, key_grad, (((0,), (0,)), ((), ())), preferred_element_type=jnp.float32
        ),
        "fsdp",
        scatter_dimension=0,
        tiled=True,
    )
    weight_grad = lax.psum(weight_shard, "dp")
    scattered = (
        jnp.zeros((group_count * capacity, model_width), jnp.bfloat16)
        .at[bucket]
        .set(pos_grad)
        .reshape(group_count, capacity, model_width)
    )
    returned = lax.all_to_all(scattered, "dp", split_axis=0, concat_axis=0, tiled=True)
    item_table = (
        requested.reshape(1, group_count * capacity)
        == lax.broadcasted_iota(jnp.int32, (item_count, group_count * capacity), 0)
    ).astype(jnp.bfloat16)
    item_grad = jnp.dot(
        item_table,
        returned.reshape(group_count * capacity, model_width),
        preferred_element_type=jnp.float32,
    )
    (tokens_back,) = pool_back(item_grad)
    token_grads = tokens_back.reshape(item_count * block_rows, model_width).astype(jnp.bfloat16)
    return (key_rows, weight_grad, token_grads)


def solution(mesh):
    in_specs = (
        P(("dp", "fsdp"), None),
        P(("dp", "fsdp")),
        P(),
        P(("dp", "fsdp"), None),
        P(("dp", "fsdp")),
        P(("dp", "fsdp")),
        P(),
        P("fsdp", None),
        P(("dp", "fsdp"), None),
    )
    out_specs = (P(("dp", "fsdp"), None), P("fsdp", None), P(("dp", "fsdp"), None))
    return jax.shard_map(local, mesh=mesh, in_specs=in_specs, out_specs=out_specs, check_vma=False)
```

profile of v0, /device:TPU:2, one launch (start us, length us, event | category | flops | bytes accessed | tf_op | source)
XLA Modules:
  0.0 447.3 jit_solution(16365344587193851670)
XLA Ops:
  7.2 0.7 all-gather.2.cloned.1.call-update
  7.9 0.7 fusion.19
  8.6 0.6 reduce-window.6
  9.4 0.8 fusion.18
  10.2 0.7 and_reduce_fusion
  10.9 1.6 scatter_custom_fusion
  12.4 0.7 all_to_all.12
  13.1 11.2 %all-to-all-start = ((s32[16,1,24]{2,1,0:T(1,128)}), s32[16,1,24]{2,1,0:T(1,128)S(1)}, u32[]{:S(2)}, u32[]{:S(2)}) async-start(s32[16,1,24]{2,1,0:T(1,128)} %all_to_all.12), calls=%async_computation | async-start | bytes 16384 | tf_op jit(solution)/shard_map/all_to_all | solution.py:65
  24.4 0.8 convert_element_type.59
  25.2 1.0 fusion.27
  26.2 3.1 multiply_reduce_fusion.1
  29.3 2.1 multiply_reduce_fusion
  31.5 2.8 all-to-all-done
  34.3 0.5 broadcast.177
  34.8 0.7 reduce.13
  35.6 4.0 gather_fusion
  39.5 4.0 broadcast_select_fusion
  43.5 6.9 %all-to-all-start.1 = ((bf16[16,24,4096]{2,1,0:T(8,128)(2,1)}), bf16[16,24,4096]{2,1,0:T(8,128)(2,1)}, u32[]{:S(2)}, u32[]{:S(2)}) async-start(bf16[16,24,4096]{2,1,0:T(8,128)(2,1)} %broadcast_select_fusion), calls=%async_computation.1 | async-start | bytes 6291456 | tf_op jit(solution)/shard_map/all_to_all | solution.py:69
  50.4 0.2 reduce-scatter.2.cloned.1.call-start
  51.3 71.9 %all-to-all-done.1 = bf16[16,24,4096]{2,1,0:T(8,128)(2,1)} async-done(((bf16[16,24,4096]{2,1,0:T(8,128)(2,1)}), bf16[16,24,4096]{2,1,0:T(8,128)(2,1)}, u32[]{:S(2)}, u32[]{:S(2)}) %all-to-all-start.1) | async-done | bytes 3145760 | tf_op jit(solution)/shard_map/all_to_all | solution.py:69
  123.2 6.2 %gather_fusion.1 = bf16[256,4096]{1,0:T(8,128)(2,1)S(1)} fusion(bf16[384,4096]{1,0:T(8,128)(2,1)} %bitcast.10, s32[1024]{0:T(1024)S(1)} %pad_clamp_fusion), kind=kCustom, calls=%fused_computation.1 | custom fusion | bytes 4195328 | tf_op jit(solution)/shard_map/jit(_take)/gather | solution.py:70
  129.4 8.3 %fusion.10 = (f32[256]{0:T(256)S(1)}, f32[256]{0:T(256)S(1)}, f32[256,4096]{1,0:T(8,128)}) fusion(bf16[256,4096]{1,0:T(8,128)(2,1)S(1)} %gather_fusion.1, pred[256]{0:T(512)(128)(4,1)S(1)} %get-tuple-element.5, pred[256]{0:T(512)(128)(4,1)S(1)} %iota_compare_fusion.5, f32[4096]{0:T(1024)S(1)} %copy-done.4, bf16[256,1024]{1,0:T(8,128)(2,1)S(1)} %copy-done, ...), kind=kOutput, calls=%fused_computation.25 | convolution fusion | flops 2155871744 | bytes 15223296 | tf_op jit(solution)/shard_map/dot_general | solution.py:79
  137.8 8.6 %fusion.13 = f32[4096,1024]{1,0:T(8,128)} fusion(bf16[256,1024]{1,0:T(8,128)(2,1)S(1)} %copy-done, f32[4096]{0:T(1024)S(1)} %copy-done.4, f32[256]{0:T(256)S(1)} %get-tuple-element.10, bf16[256,4096]{1,0:T(8,128)(2,1)S(1)} %gather_fusion.1, pred[256]{0:T(512)(128)(4,1)S(1)} %get-tuple-element.5, pred[256]{0:T(512)(128)(4,1)S(1)} %iota_compare_fusion.5), kind=kOutput, calls=%fused_computation.31 | convolution fusion | flops 2153775104 | bytes 19416576 | tf_op jit(solution)/shard_map/dot_general | solution.py:85
  146.4 8.3 %scatter_custom_fusion.1 = bf16[384,4096]{1,0:T(8,128)(2,1)} fusion(s32[256]{0:T(256)S(1)} %bitcast.64, bf16[]{:T(256)} %constant.57.clone.1, f32[256,4096]{1,0:T(8,128)} %get-tuple-element.13, f32[256]{0:T(256)S(1)} %get-tuple-element.9, f32[256]{0:T(256)S(1)} %get-tuple-element.10, pred[256]{0:T(512)(128)(4,1)S(1)} %iota_compare_fusion.5, ...), kind=kCustom, calls=%fused_computation.28 | custom fusion | flops 9437184 | bytes 9440258 | tf_op jit(solution)/shard_map/scatter | solution.py:96
  154.7 8.9 %all-to-all-start.2 = ((bf16[16,24,4096]{2,1,0:T(8,128)(2,1)}), bf16[16,24,4096]{2,1,0:T(8,128)(2,1)}, u32[]{:S(2)}, u32[]{:S(2)}) async-start(bf16[16,24,4096]{2,1,0:T(8,128)(2,1)} %bitcast.57), calls=%async_computation.3 | async-start | bytes 6291456 | tf_op jit(solution)/shard_map/all_to_all | solution.py:99
  163.8 108.0 %reduce-scatter.2.cloned.1.call-done = f32[256,1024]{1,0:T(8,128)} async-done(((f32[4096,1024]{1,0:T(8,128)}), f32[256,1024]{1,0:T(8,128)}) %reduce-scatter.2.cloned.1.call-update) | async-done | bytes 1048592 | tf_op jit(solution)/shard_map/reduce_scatter | solution.py:84
  271.8 6.6 %convolution_convert_fusion = bf16[256,1024]{1,0:T(8,128)(2,1)} fusion(bf16[4096,1024]{1,0:T(8,128)(2,1)} %all-gather.2.cloned.1.call-done, f32[4096]{0:T(1024)S(1)} %copy-done.4, f32[256]{0:T(256)S(1)} %get-tuple-element.10, bf16[256,4096]{1,0:T(8,128)(2,1)S(1)} %gather_fusion.1, pred[256]{0:T(512)(128)(4,1)S(1)} %get-tuple-element.5, ...), kind=kOutput, calls=%fused_computation.30 | convolution fusion | flops 2154037248 | bytes 11027968 | tf_op jit(solution)/shard_map/dot_general | solution.py:78
  278.5 2.6 convolution_divide_fusion
  281.0 3.7 fusion.4
  284.7 4.3 fusion
  289.0 149.5 %all-reduce.2.cloned.1.call-done = f32[256,1024]{1,0:T(8,128)} async-done(((f32[256,1024]{1,0:T(8,128)}), f32[256,1024]{1,0:T(8,128)}) %all-reduce.2.cloned.1.call-update) | async-done | bytes 1048592 | tf_op jit(solution)/shard_map/psum | solution.py:92
  438.5 2.3 copy.18
  (30 shorter events, 0.7 us)
Async XLA Ops:
  7.2 122.3 %copy-start = (bf16[256,1024]{1,0:T(8,128)(2,1)S(1)}, bf16[256,1024]{1,0:T(8,128)(2,1)}, u32[]{:S(2)}) copy-start(bf16[256,1024]{1,0:T(8,128)(2,1)} %param.17) | copy-start | bytes 1572868
  7.2 22.1 %copy-start.3 = (f32[4096]{0:T(1024)S(1)}, f32[4096]{0:T(1024)}, u32[]{:S(2)}) copy-start(f32[4096]{0:T(1024)} %param.11) | copy-start | bytes 49156
  7.2 122.2 %all-gather.2.cloned.1.call-start = ((), (), s32[]{:S(2)}) async-start(), calls=%async_computation.4 | async-start | bytes 8912896 | tf_op jit(solution)/shard_map/all_gather | solution.py:44
  13.1 21.1 %all-to-all-start = ((s32[16,1,24]{2,1,0:T(1,128)}), s32[16,1,24]{2,1,0:T(1,128)S(1)}, u32[]{:S(2)}, u32[]{:S(2)}) async-start(s32[16,1,24]{2,1,0:T(1,128)} %all_to_all.12), calls=%async_computation | async-start | bytes 16384 | tf_op jit(solution)/shard_map/all_to_all | solution.py:65
  24.4 4.9 %copy-start.1 = (bf16[512,4096]{1,0:T(8,128)(2,1)S(1)}, bf16[512,4096]{1,0:T(8,128)(2,1)}, u32[]{:S(2)}) copy-start(bf16[512,4096]{1,0:T(8,128)(2,1)} %param.9) | copy-start | bytes 12582916
  43.5 79.7 %all-to-all-start.1 = ((bf16[16,24,4096]{2,1,0:T(8,128)(2,1)}), bf16[16,24,4096]{2,1,0:T(8,128)(2,1)}, u32[]{:S(2)}, u32[]{:S(2)}) async-start(bf16[16,24,4096]{2,1,0:T(8,128)(2,1)} %broadcast_select_fusion), calls=%async_computation.1 | async-start | bytes 6291456 | tf_op jit(solution)/shard_map/all_to_all | solution.py:69
  50.4 221.4 %reduce-scatter.2.cloned.1.call-start = ((), (), s32[]{:S(2)}) async-start(), calls=%async_computation.5 | async-start | bytes 17825792 | tf_op jit(solution)/shard_map/reduce_scatter | solution.py:84
  123.2 6.2 %copy-start.4 = (f32[4096]{0:T(1024)S(1)}, f32[4096]{0:T(1024)}, u32[]{:S(2)}) copy-start(f32[4096]{0:T(1024)} %param.15) | copy-start | bytes 49156
  154.7 123.8 %all-to-all-start.2 = ((bf16[16,24,4096]{2,1,0:T(8,128)(2,1)}), bf16[16,24,4096]{2,1,0:T(8,128)(2,1)}, u32[]{:S(2)}, u32[]{:S(2)}) async-start(bf16[16,24,4096]{2,1,0:T(8,128)(2,1)} %bitcast.57), calls=%async_computation.3 | async-start | bytes 6291456 | tf_op jit(solution)/shard_map/all_to_all | solution.py:99
  163.6 274.8 %all-reduce.2.cloned.1.call-start = ((), (), s32[]{:S(2)}) async-start(), calls=%async_computation.6 | async-start | bytes 2097152 | tf_op jit(solution)/shard_map/psum | solution.py:92
  278.5 6.3 %copy-start.2 = (bf16[512,4096]{1,0:T(8,128)(2,1)S(1)}, bf16[512,4096]{1,0:T(8,128)(2,1)}, u32[]{:S(2)}) copy-start(bf16[512,4096]{1,0:T(8,128)(2,1)} %param.9) | copy-start | bytes 12582916
Sparse Core Ops, SparseCore 0:
  9.9 68.8 all-gather.1
  146.5 125.2 reduce-scatter.1
  274.5 163.9 all-reduce.1
where the time goes:
time: 448 us; the launch traced here: 447 us
  waiting for transfers between devices  333 us (74%)
  other arithmetic  30.8 us (7%)
  starting transfers between devices  27.3 us (6%)
  matrix products  26 us (6%)
  local copies, waits for them, and re-layouts  15.6 us (3%)
  between operations  14.6 us (3%)
    psum x1, waiting for transfers between devices, local(): weight_grad = lax.psum(weight_shard, 'dp')  149 us
    reduce_scatter x1, waiting for transfers between devices, local(): lax.psum_scatter(lax.dot_general(hidden, key_grad, (((0,), (0,)), ((), ()...  108 us
    all_to_all x1, waiting for transfers between devices, local(): lax.all_to_all(outgoing, 'dp', split_axis=0, concat_axis=0, tiled=True)  71.9 us
    all_to_all x1, starting transfers between devices, local(): lax.all_to_all(request, 'dp', split_axis=0, concat_axis=0, tiled=True)  11.2 us
  transfers between devices with their start and end apart: 6, of which 4 were waited for; matrix products, arithmetic and copies ran while one was open for 12% of the time, Pallas kernels for 0%

commit v1 on v0

--- a/solution.py
+++ b/solution.py
@@ -89,7 +89,7 @@
         scatter_dimension=0,
         tiled=True,
     )
-    weight_grad = lax.psum(weight_shard, "dp")
+    weight_grad = jnp.sum(lax.all_gather(weight_shard, "dp"), axis=0)
     scattered = (
         jnp.zeros((group_count * capacity, model_width), jnp.bfloat16)
         .at[bucket]

time: 448 us -> 555 us (1.24)
  waiting for transfers between devices: 333 us -> 432 us
  other arithmetic: 30.8 us -> 39.4 us
    all_gather x0 -> x1, waiting for transfers between devices: none -> 159 us  [local(): weight_grad = jnp.sum(lax.all_gather(weight_shard, 'dp'), axis=0)]
    psum x1 -> x0, waiting for transfers between devices: 149 us -> none  [local(): weight_grad = lax.psum(weight_shard, 'dp')]
    all_to_all x1, waiting for transfers between devices: 0.01 us -> 99.7 us  [local(): lax.all_to_all(scattered, 'dp', split_axis=0, concat_axis=0, tiled=True)]
    reduce_scatter x1, waiting for transfers between devices: 108 us -> 98.1 us  [local(): lax.psum_scatter(lax.dot_general(hidden, key_grad, (((0,), (0,)), ((), ()...]
    reduce_sum x0 -> x1, other arithmetic: none -> 8.76 us  [local(): weight_grad = jnp.sum(lax.all_gather(weight_shard, 'dp'), axis=0)]
  transfers between devices with their start and end apart: 6 -> 6, of which waited for: 4 -> 5; matrix products, arithmetic and copies ran while one was open for 12% -> 10% of each run, Pallas kernels for 0% -> 0%
where the time goes in v1:
time: 555 us; the launch traced here: 554 us
  waiting for transfers between devices  432 us (78%)
  other arithmetic  39.4 us (7%)
  starting transfers between devices  28.4 us (5%)
  matrix products  26.5 us (5%)
  between operations  14.6 us (3%)
  local copies, waits for them, and re-layouts  13.3 us (2%)
    all_gather x1, waiting for transfers between devices, local(): weight_grad = jnp.sum(lax.all_gather(weight_shard, 'dp'), axis=0)  159 us
    all_to_all x1, waiting for transfers between devices, local(): lax.all_to_all(scattered, 'dp', split_axis=0, concat_axis=0, tiled=True)  99.7 us
    reduce_scatter x1, waiting for transfers between devices, local(): lax.psum_scatter(lax.dot_general(hidden, key_grad, (((0,), (0,)), ((), ()...  98.1 us
    all_to_all x1, waiting for transfers between devices, local(): lax.all_to_all(outgoing, 'dp', split_axis=0, concat_axis=0, tiled=True)  71.9 us
    all_to_all x1, starting transfers between devices, local(): lax.all_to_all(request, 'dp', split_axis=0, concat_axis=0, tiled=True)  11.2 us
  transfers between devices with their start and end apart: 6, of which 5 were waited for; matrix products, arithmetic and copies ran while one was open for 10% of the time, Pallas kernels for 0%

profile of v1, /device:TPU:2, one launch (start us, length us, event | category | flops | bytes accessed | tf_op | source)
XLA Modules:
  0.0 554.0 jit_solution(1006804259427630792)
XLA Ops:
  7.2 0.7 all-gather.4.cloned.1.call-update
  7.9 0.7 fusion.19
  8.6 0.6 reduce-window.6
  9.4 0.8 fusion.18
  10.2 0.7 and_reduce_fusion
  10.9 1.6 scatter_custom_fusion
  12.4 0.7 all_to_all.12
  13.1 11.2 %all-to-all-start = ((s32[16,1,24]{2,1,0:T(1,128)}), s32[16,1,24]{2,1,0:T(1,128)S(1)}, u32[]{:S(2)}, u32[]{:S(2)}) async-start(s32[16,1,24]{2,1,0:T(1,128)} %all_to_all.12), calls=%async_computation | async-start | bytes 16384 | tf_op jit(solution)/shard_map/all_to_all | solution.py:65
  24.4 0.8 convert_element_type.59
  25.2 1.0 fusion.27
  26.2 3.1 multiply_reduce_fusion.1
  29.3 2.1 multiply_reduce_fusion
  31.5 2.8 all-to-all-done
  34.3 0.5 broadcast.177
  34.8 0.7 reduce.13
  35.6 4.0 gather_fusion
  39.5 4.0 broadcast_select_fusion
  43.5 6.9 %all-to-all-start.1 = ((bf16[16,24,4096]{2,1,0:T(8,128)(2,1)}), bf16[16,24,4096]{2,1,0:T(8,128)(2,1)}, u32[]{:S(2)}, u32[]{:S(2)}) async-start(bf16[16,24,4096]{2,1,0:T(8,128)(2,1)} %broadcast_select_fusion), calls=%async_computation.1 | async-start | bytes 6291456 | tf_op jit(solution)/shard_map/all_to_all | solution.py:69
  51.3 71.9 %all-to-all-done.1 = bf16[16,24,4096]{2,1,0:T(8,128)(2,1)} async-done(((bf16[16,24,4096]{2,1,0:T(8,128)(2,1)}), bf16[16,24,4096]{2,1,0:T(8,128)(2,1)}, u32[]{:S(2)}, u32[]{:S(2)}) %all-to-all-start.1) | async-done | bytes 3145760 | tf_op jit(solution)/shard_map/all_to_all | solution.py:69
  123.2 6.2 %gather_fusion.1 = bf16[256,4096]{1,0:T(8,128)(2,1)S(1)} fusion(bf16[384,4096]{1,0:T(8,128)(2,1)} %bitcast.10, s32[1024]{0:T(1024)S(1)} %pad_clamp_fusion), kind=kCustom, calls=%fused_computation.1 | custom fusion | bytes 4195328 | tf_op jit(solution)/shard_map/jit(_take)/gather | solution.py:70
  129.4 8.3 %fusion.10 = (f32[256]{0:T(256)S(1)}, f32[256]{0:T(256)S(1)}, f32[256,4096]{1,0:T(8,128)}) fusion(bf16[256,4096]{1,0:T(8,128)(2,1)S(1)} %gather_fusion.1, pred[256]{0:T(512)(128)(4,1)S(1)} %get-tuple-element.5, pred[256]{0:T(512)(128)(4,1)S(1)} %iota_compare_fusion.5, f32[4096]{0:T(1024)S(1)} %copy-done.5, bf16[256,1024]{1,0:T(8,128)(2,1)S(1)} %copy-done, ...), kind=kOutput, calls=%fused_computation.25 | convolution fusion | flops 2155871744 | bytes 15223296 | tf_op jit(solution)/shard_map/dot_general | solution.py:79
  137.8 8.6 %fusion.13 = f32[4096,1024]{1,0:T(8,128)} fusion(bf16[256,1024]{1,0:T(8,128)(2,1)S(1)} %copy-done, f32[4096]{0:T(1024)S(1)} %copy-done.5, f32[256]{0:T(256)S(1)} %get-tuple-element.10, bf16[256,4096]{1,0:T(8,128)(2,1)S(1)} %gather_fusion.1, pred[256]{0:T(512)(128)(4,1)S(1)} %get-tuple-element.5, pred[256]{0:T(512)(128)(4,1)S(1)} %iota_compare_fusion.5), kind=kOutput, calls=%fused_computation.31 | convolution fusion | flops 2153775104 | bytes 19416576 | tf_op jit(solution)/shard_map/dot_general | solution.py:85
  146.6 98.1 %reduce-scatter.2.cloned.1.call-done = f32[256,1024]{1,0:T(8,128)} async-done(((f32[4096,1024]{1,0:T(8,128)}), f32[256,1024]{1,0:T(8,128)}) %reduce-scatter.2.cloned.1.call-update) | async-done | bytes 1048592 | tf_op jit(solution)/shard_map/reduce_scatter | solution.py:84
  244.8 8.1 %scatter_custom_fusion.1 = bf16[384,4096]{1,0:T(8,128)(2,1)} fusion(s32[256]{0:T(256)S(1)} %bitcast.66, bf16[]{:T(256)} %constant.57.clone.1, f32[256,4096]{1,0:T(8,128)} %get-tuple-element.13, f32[256]{0:T(256)S(1)} %get-tuple-element.9, f32[256]{0:T(256)S(1)} %get-tuple-element.10, pred[256]{0:T(512)(128)(4,1)S(1)} %iota_compare_fusion.5, ...), kind=kCustom, calls=%fused_computation.28 | custom fusion | flops 9437184 | bytes 9440258 | tf_op jit(solution)/shard_map/scatter | solution.py:96
  252.9 9.8 %all-to-all-start.2 = ((bf16[16,24,4096]{2,1,0:T(8,128)(2,1)}), bf16[16,24,4096]{2,1,0:T(8,128)(2,1)}, u32[]{:S(2)}, u32[]{:S(2)}) async-start(bf16[16,24,4096]{2,1,0:T(8,128)(2,1)} %bitcast.59), calls=%async_computation.3 | async-start | bytes 6291456 | tf_op jit(solution)/shard_map/all_to_all | solution.py:99
  262.8 7.0 %convolution_convert_fusion = bf16[256,1024]{1,0:T(8,128)(2,1)} fusion(bf16[4096,1024]{1,0:T(8,128)(2,1)} %all-gather.4.cloned.1.call-done, f32[4096]{0:T(1024)S(1)} %copy-done.5, f32[256]{0:T(256)S(1)} %get-tuple-element.10, bf16[256,4096]{1,0:T(8,128)(2,1)S(1)} %gather_fusion.1, pred[256]{0:T(512)(128)(4,1)S(1)} %get-tuple-element.5, ...), kind=kOutput, calls=%fused_computation.30 | convolution fusion | flops 2154037248 | bytes 11027968 | tf_op jit(solution)/shard_map/dot_general | solution.py:78
  269.8 99.7 %all-to-all-done.2 = bf16[16,24,4096]{2,1,0:T(8,128)(2,1)} async-done(((bf16[16,24,4096]{2,1,0:T(8,128)(2,1)}), bf16[16,24,4096]{2,1,0:T(8,128)(2,1)}, u32[]{:S(2)}, u32[]{:S(2)}) %all-to-all-start.2) | async-done | bytes 3145760 | tf_op jit(solution)/shard_map/all_to_all | solution.py:99
  369.6 2.6 convolution_divide_fusion
  372.1 3.7 fusion.4
  375.8 4.3 fusion
  380.1 158.5 %all-gather.6.cloned.1.call-done = f32[4096,1024]{1,0:T(8,128)} async-done(((f32[256,1024]{1,0:T(8,128)}), f32[4096,1024]{1,0:T(8,128)}) %all-gather.6.cloned.1.call-update) | async-done | bytes 16777232 | tf_op jit(solution)/shard_map/all_gather | solution.py:92
  538.7 8.8 %reduce_sum.78 = f32[256,1024]{1,0:T(8,128)} reduce(f32[16,256,1024]{2,1,0:T(8,128)} %bitcast.57, f32[]{:T(128)} %constant.32.clone.1), dimensions={0}, to_apply=%region_8.9 | reduce | flops 3932160 | bytes 17825796 | tf_op jit(solution)/shard_map/reduce_sum | solution.py:92
  (32 shorter events, 1.2 us)
Async XLA Ops:
  7.2 122.3 %copy-start = (bf16[256,1024]{1,0:T(8,128)(2,1)S(1)}, bf16[256,1024]{1,0:T(8,128)(2,1)}, u32[]{:S(2)}) copy-start(bf16[256,1024]{1,0:T(8,128)(2,1)} %param.17) | copy-start | bytes 1572868
  7.2 22.1 %copy-start.4 = (f32[4096]{0:T(1024)S(1)}, f32[4096]{0:T(1024)}, u32[]{:S(2)}) copy-start(f32[4096]{0:T(1024)} %param.11) | copy-start | bytes 49156
  7.2 122.2 %all-gather.4.cloned.1.call-start = ((), (), s32[]{:S(2)}) async-start(), calls=%async_computation.4 | async-start | bytes 8912896 | tf_op jit(solution)/shard_map/all_gather | solution.py:44
  13.1 21.1 %all-to-all-start = ((s32[16,1,24]{2,1,0:T(1,128)}), s32[16,1,24]{2,1,0:T(1,128)S(1)}, u32[]{:S(2)}, u32[]{:S(2)}) async-start(s32[16,1,24]{2,1,0:T(1,128)} %all_to_all.12), calls=%async_computation | async-start | bytes 16384 | tf_op jit(solution)/shard_map/all_to_all | solution.py:65
  24.4 4.9 copy-start.2
  43.5 79.7 %all-to-all-start.1 = ((bf16[16,24,4096]{2,1,0:T(8,128)(2,1)}), bf16[16,24,4096]{2,1,0:T(8,128)(2,1)}, u32[]{:S(2)}, u32[]{:S(2)}) async-start(bf16[16,24,4096]{2,1,0:T(8,128)(2,1)} %broadcast_select_fusion), calls=%async_computation.1 | async-start | bytes 6291456 | tf_op jit(solution)/shard_map/all_to_all | solution.py:69
  50.4 194.4 %reduce-scatter.2.cloned.1.call-start = ((), (), s32[]{:S(2)}) async-start(), calls=%async_computation.5 | async-start | bytes 17825792 | tf_op jit(solution)/shard_map/reduce_scatter | solution.py:84
  123.2 6.2 %copy-start.5 = (f32[4096]{0:T(1024)S(1)}, f32[4096]{0:T(1024)}, u32[]{:S(2)}) copy-start(f32[4096]{0:T(1024)} %param.15) | copy-start | bytes 49156
  146.4 392.3 %all-gather.6.cloned.1.call-start = ((), (), s32[]{:S(2)}) async-start(), calls=%async_computation.6 | async-start | bytes 17825792 | tf_op jit(solution)/shard_map/all_gather | solution.py:92
  252.9 116.7 %all-to-all-start.2 = ((bf16[16,24,4096]{2,1,0:T(8,128)(2,1)}), bf16[16,24,4096]{2,1,0:T(8,128)(2,1)}, u32[]{:S(2)}, u32[]{:S(2)}) async-start(bf16[16,24,4096]{2,1,0:T(8,128)(2,1)} %bitcast.59), calls=%async_computation.3 | async-start | bytes 6291456 | tf_op jit(solution)/shard_map/all_to_all | solution.py:99
  369.6 6.3 %copy-start.3 = (bf16[512,4096]{1,0:T(8,128)(2,1)S(1)}, bf16[512,4096]{1,0:T(8,128)(2,1)}, u32[]{:S(2)}) copy-start(bf16[512,4096]{1,0:T(8,128)(2,1)} %param.9) | copy-start | bytes 12582916
  538.7 8.8 %copy-start.1 = (bf16[256,1024]{1,0:T(8,128)(2,1)S(1)}, bf16[256,1024]{1,0:T(8,128)(2,1)}, u32[]{:S(2)}) copy-start(bf16[256,1024]{1,0:T(8,128)(2,1)} %param.17) | copy-start | bytes 1572868
Sparse Core Ops, SparseCore 0:
  9.8 68.8 all-gather.3
  146.5 98.2 reduce-scatter.1
  247.3 291.2 all-gather.5
